TPU v7x, 256 devices: a whole 4x4x8 slice. The times are simulated.
256 devices in a mesh: member: 64 (over z_lo, x, y, core), shard: 4 (over z_hi).
Axes of the slice: x: 4, y: 4, z: 8 (z_hi: 4, z_lo: 2; z = z_hi * 2 + z_lo), core: 2. Of those that a mesh axis runs over, the one named last changes fastest.
Arguments:
- processor_latent: bfloat16 [64, 128, 1024], P('member', 'shard'), may hold values from -240 to 240
- stencil_index: int32 [4, 3, 768], P('shard'), may hold values from 0 to 127
- interp_weight: float32 [4, 3, 768], P('shard'), may hold values from 0.1 to 1
- prev_state: float32 [4, 112, 768], P('shard'), may hold values from -6 to 6
- observed: float32 [4, 112, 768], P('shard', None, 'member'), may hold values from -6 to 6
- cell_area: float32 [4, 768], P('shard', 'member'), may hold values from 0.5 to 2
- var_weight: float32 [112], replicated, may hold values from 1 to 16
- hidden_weight: bfloat16 [1024, 1024], replicated, may hold values from -0.1875 to 0.1875
- hidden_bias: float32 [1024], replicated, may hold values from -3 to 3
- output_weight: bfloat16 [1024, 112], replicated, may hold values from -0.1875 to 0.1875
- output_bias: float32 [112], replicated, may hold values from -3 to 3
Outputs:
- mesh_grad: float32 [64, 128, 1024], P('member', 'shard')
Inputs may be any that keep to these rules, and one draw needn't show every extreme that they name: `stencil_index`: rows of the same member's mesh.
All inputs are finite; a program needn't handle non-finite values.
Results may differ from a plain program's by a relative error of at most 0.019.
Values may be sent and summed in bfloat16 or wider, within the bound.
A program may use at most 64 MiB of HBM per device.

v0:
```python
import jax
import jax.numpy as jnp
from jax import lax
from jax.sharding import PartitionSpec as P

smoothing = 0.05
fairness = 0.95
epsilon = 1e-05


def softened_slope(differ):
    return differ / jnp.sqrt(differ * differ + smoothing * smoothing)


def normalize(latent):
    average = jnp.mean(latent, axis=1, keepdims=True)
    centred = latent - average
    inverse = lax.rsqrt(jnp.mean(centred * centred, axis=1, keepdims=True) + epsilon)
    return (centred * inverse, inverse)


def stencil_matrix(stencil, weights, row_count):
    row_ids = lax.iota(jnp.int32, row_count)
    hits = stencil[:, :, None] == row_ids[None, None, :]
    return jnp.sum(jnp.where(hits, weights[:, :, None], 0.0), axis=0)


def decode_members(normed, hidden_weight, hidden_bias, output_weight, output_bias, previous):
    pre_act = jnp.dot(normed, hidden_weight, preferred_element_type=jnp.float32) + hidden_bias
    hidden = jax.nn.silu(pre_act).astype(jnp.bfloat16)
    update = lax.dot_general(
        output_weight, hidden, (((0,), (1,)), ((), ())), preferred_element_type=jnp.float32
    )
    return (previous + (update + output_bias[:, None]), pre_act)


def local(
    processor_latent,
    stencil_index,
    interp_weight,
    prev_state,
    observed,
    cell_area,
    var_weight,
    hidden_weight,
    hidden_bias,
    output_weight,
    output_bias,
):
    mesh_local = processor_latent[0]
    stencil = stencil_index[0]
    weights = interp_weight[0]
    previous = prev_state[0]
    cell_count = stencil.shape[1]
    features = mesh_local.shape[1]
    variables = previous.shape[0]
    members = lax.axis_size("member")
    block_cells = cell_count // members
    shard_rows = lax.all_gather(mesh_local, "shard", axis=0, tiled=True)
    matrix = stencil_matrix(stencil, weights, shard_rows.shape[0])
    latent = jnp.dot(
        matrix,
        shard_rows.astype(jnp.float32),
        precision=lax.Precision.HIGHEST,
        preferred_element_type=jnp.float32,
    )
    normal_form, inverse = normalize(latent)
    normed = normal_form.astype(jnp.bfloat16)
    fairness_factor = (1.0 - fairness) / members
    bounds = (0, block_cells)
    arranged = normed.reshape(members, block_cells, features)
    earlier = previous.reshape(variables, members, block_cells)
    first_cell, stop_cell = bounds
    width_part = stop_cell - first_cell
    piece_rows = arranged.reshape(-1, features)
    prior_piece = earlier.reshape(variables, -1)
    prediction_piece, preactivation_piece = decode_members(
        piece_rows, hidden_weight, hidden_bias, output_weight, output_bias, prior_piece
    )
    received = lax.all_to_all(
        prediction_piece[None], "member", split_axis=2, concat_axis=0, tiled=True
    )
    stored = preactivation_piece.reshape(members, width_part, -1)
    pre_act = stored.reshape(cell_count, -1)
    flattened = received.reshape(members, -1)
    groups = flattened.reshape(members // 8, 8, -1)

    def group_pairs(chosen):
        return jnp.sum(softened_slope(chosen[:, None] - flattened[None]), axis=1)

    pairwise_sums = lax.map(group_pairs, groups).reshape(received.shape)
    loss_weighting = cell_area[0][None, None, :] * var_weight[None, :, None]
    slopes = (
        loss_weighting
        * (
            softened_slope(received - observed[0][None])
            - (1.0 - fairness_factor) / (members - 1) * pairwise_sums
        )
    ).astype(jnp.bfloat16)
    upstream_gradient = lax.all_to_all(slopes, "member", split_axis=0, concat_axis=2, tiled=True)[0]
    grad_hidden = lax.dot_general(
        upstream_gradient,
        output_weight,
        (((0,), (1,)), ((), ())),
        preferred_element_type=jnp.float32,
    )
    logistic = jax.nn.sigmoid(pre_act)
    grad_pre = (grad_hidden * (logistic * (1.0 + pre_act * (1.0 - logistic)))).astype(jnp.bfloat16)
    grad_normed = lax.dot_general(
        grad_pre, hidden_weight, (((1,), (1,)), ((), ())), preferred_element_type=jnp.float32
    )
    grad_cell = inverse * (
        grad_normed
        - jnp.mean(grad_normed, axis=1, keepdims=True)
        - normal_form * jnp.mean(grad_normed * normal_form, axis=1, keepdims=True)
    )
    matrix = stencil_matrix(stencil, weights, lax.axis_size("shard") * mesh_local.shape[0])
    mesh_grad = lax.psum_scatter(
        lax.dot_general(
            matrix,
            grad_cell,
            (((0,), (0,)), ((), ())),
            precision=lax.Precision.HIGHEST,
            preferred_element_type=jnp.float32,
        ).astype(jnp.bfloat16),
        "shard",
        scatter_dimension=0,
        tiled=True,
    ).astype(jnp.float32)
    return mesh_grad[None]


def solution(mesh):
    in_specs = (
        P("member", "shard", None),
        P("shard", None, None),
        P("shard", None, None),
        P("shard", None, None),
        P("shard", None, "member"),
        P("shard", "member"),
        P(),
        P(),
        P(),
        P(),
        P(),
    )
    out_specs = P("member", "shard", None)
    return jax.shard_map(local, mesh=mesh, in_specs=in_specs, out_specs=out_specs, check_vma=False)
```

profile of v0, /device:TPU:2, one launch (start us, length us, event | category | flops | bytes accessed | tf_op | source)
XLA Modules:
  0.0 147.1 jit_solution(18232021255405809372)
XLA Ops:
  6.5 0.9 copy.50
  8.1 18.1 %all-gather = bf16[1,128,1024]{2,1,0:T(8,128)(2,1)S(1)} all-gather(bf16[1,32,1024]{2,1,0:T(8,128)(2,1)} %param.13), channel_id=2, replica_groups=mesh['member'=64,'shard'=4] {'shard'}, dimensions={1}, use_global_device_ids=true | all-gather | bytes 327680 | tf_op jit(solution)/shard_map/all_gather | solution.py:59
  26.2 0.8 select_reduce_fusion
  27.0 0.7 copy-done.2
  27.7 1.5 %fusion.31 = (f32[768]{0:T(1024)S(1)}, f32[768,1024]{1,0:T(8,128)S(1)}) fusion(f32[768,128]{1,0:T(8,128)S(1)} %select_reduce_fusion, bf16[1,128,1024]{2,1,0:T(8,128)(2,1)S(1)} %all-gather), kind=kOutput, calls=%fused_computation.52 | convolution fusion | flops 1208745216 | bytes 3804160 | tf_op jit(solution)/shard_map/dot_general | solution.py:61
  29.8 1.9 %fusion.9 = f32[768,1024]{1,0:T(8,128)S(1)} fusion(bf16[1024,1024]{1,0:T(8,128)(2,1)S(1)} %copy-done, f32[768,1024]{1,0:T(8,128)S(1)} %get-tuple-element.55, f32[768]{0:T(1024)S(1)} %add_rsqrt_fusion, f32[768]{0:T(1024)S(1)} %broadcast_multiply_fusion.4), kind=kOutput, calls=%fused_computation.19 | convolution fusion | flops 1612972032 | bytes 8394752 | tf_op jit(solution)/shard_map/dot_general | solution.py:29
  31.7 1.7 %copy-done.14 = f32[768,1024]{1,0:T(8,128)} copy-done((f32[768,1024]{1,0:T(8,128)}, f32[768,1024]{1,0:T(8,128)S(1)}, u32[]{:S(2)}) %copy-start.14) | copy-done | bytes 3145752
  33.4 1.1 fusion.25
  34.5 1.0 copy.34
  35.5 8.5 %all-to-all-start = ((f32[1,112,768]{1,0,2:T(1,128)}), f32[1,112,768]{1,0,2:T(1,128)S(1)}, u32[]{:S(2)}, u32[]{:S(2)}) async-start(f32[1,112,768]{1,0,2:T(1,128)} %copy.34), calls=%async_computation | async-start | bytes 786432 | tf_op jit(solution)/shard_map/all_to_all | solution.py:80
  44.8 8.8 %all-to-all-done = f32[1,112,768]{1,0,2:T(1,128)S(1)} async-done(((f32[1,112,768]{1,0,2:T(1,128)}), f32[1,112,768]{1,0,2:T(1,128)S(1)}, u32[]{:S(2)}, u32[]{:S(2)}) %all-to-all-start) | async-done | bytes 344096 | tf_op jit(solution)/shard_map/all_to_all | solution.py:80
  53.6 3.3 %copy.36 = f32[64,1,112,12]{3,2,0,1:T(8,128)} copy(f32[64,1,112,12]{2,1,3,0:T(1,128)S(1)} %bitcast.64) | data formatting | bytes 688128 | tf_op jit(solution)/shard_map/all_to_all | solution.py:80
  56.9 1.3 copy.40
  58.2 3.8 %reshape_reshape.3 = f32[8,8,1344]{2,1,0:T(8,128)} reshape(f32[64,1,112,12]{3,2,0,1:T(8,128)} %copy.36) | data formatting | bytes 688128 | tf_op jit(solution)/shard_map/reshape;reshape | solution.py:86
  62.0 1.2 sub.126
  63.2 18.5 %while.11 = (s32[]{:T(128)}, f32[8,8,1344]{2,1,0:T(8,128)}, f32[8,8,1344]{2,1,0:T(8,128)}, f32[64,112,12]{0,2,1:T(8,128)}, f32[64,1344]{0,1:T(8,128)S(1)}, /*index=5*/s32[]{:T(128)}) while((s32[]{:T(128)}, f32[8,8,1344]{2,1,0:T(8,128)}, f32[8,8,1344]{2,1,0:T(8,128)}, f32[64,112,12]{0,2,1:T(8,128)}, f32[64,1344]{0,1:T(8,128)S(1)}, ...), condition=%wide.wide.region_5.6_spmd, body=%wide.wide.region_3.5_spmd.sunk | while | flops 3429890 | bytes 1292373 | solution.py:91
  63.5 0.8 dynamic-slice_bitcast_fusion.3
  65.8 0.8 dynamic-slice_bitcast_fusion.3
  68.1 0.8 dynamic-slice_bitcast_fusion.3
  70.4 0.8 dynamic-slice_bitcast_fusion.3
  72.7 0.8 dynamic-slice_bitcast_fusion.3
  75.0 0.8 dynamic-slice_bitcast_fusion.3
  77.4 0.8 dynamic-slice_bitcast_fusion.3
  79.7 0.8 dynamic-slice_bitcast_fusion.3
  81.7 1.0 broadcast_multiply_fusion
  82.8 3.9 %mul.93 = f32[64,112,12]{2,1,0:T(8,128)} reshape(f32[8,8,1344]{2,1,0:T(8,128)S(1)} %broadcast_multiply_fusion) | data formatting | bytes 688128 | tf_op jit(solution)/shard_map/mul | solution.py:97
  86.7 2.7 %copy.38 = f32[64,112,12]{1,0,2:T(8,128)S(1)} copy(f32[64,112,12]{2,1,0:T(8,128)} %mul.93) | data formatting | bytes 688128 | tf_op jit(solution)/shard_map/mul | solution.py:97
  89.7 13.7 %all_to_all.33 = bf16[64,112,12]{1,2,0:T(8,128)(2,1)S(1)} all-to-all(bf16[64,112,12]{1,2,0:T(8,128)(2,1)S(1)} %copy.39), channel_id=1, replica_groups=mesh['member'=64,'shard'=4] {'member'}, dimensions={0} | all-to-all | bytes 344064 | tf_op jit(solution)/shard_map/all_to_all | solution.py:100
  103.5 6.1 %fusion.30 = (f32[768]{0:T(1024)S(1)}, f32[768]{0:T(1024)S(1)}, f32[768,1024]{1,0:T(8,128)}) fusion(f32[768]{0:T(1024)S(1)} %add_rsqrt_fusion, f32[768,1024]{1,0:T(8,128)} %copy-done.1, f32[768]{0:T(1024)S(1)} %broadcast_multiply_fusion.4, bf16[1024,1024]{1,0:T(8,128)(2,1)S(1)} %copy-done, f32[768,1024]{1,0:T(8,128)} %copy-done.14, ...), kind=kOutput, calls=%fused_computation.51 | convolution fusion | flops 1798568448 | bytes 11952128 | tf_op jit(solution)/shard_map/dot_general | solution.py:109
  109.7 6.2 %fusion.19 = bf16[128,1024]{1,0:T(8,128)(2,1)} fusion(f32[768,128]{1,0:T(8,128)S(1)} %copy-done.3, f32[768,1024]{1,0:T(8,128)} %get-tuple-element.56, f32[768,1024]{1,0:T(8,128)} %copy-done.1, f32[768]{0:T(1024)S(1)} %get-tuple-element.57, f32[768]{0:T(1024)S(1)} %get-tuple-element.58, f32[768]{0:T(1024)S(1)} %add_rsqrt_fusion, ...), kind=kOutput, calls=%fused_computation.28 | convolution fusion | flops 1212809216 | bytes 6959104 | tf_op jit(solution)/shard_map/dot_general | solution.py:119
  115.9 22.9 %reduce-scatter.2.cloned.1.call-done = bf16[32,1024]{1,0:T(8,128)(2,1)} async-done(((bf16[128,1024]{1,0:T(8,128)(2,1)}), bf16[32,1024]{1,0:T(8,128)(2,1)}) %reduce-scatter.2.cloned.1.call-update) | async-done | bytes 65552 | tf_op jit(solution)/shard_map/reduce_scatter | solution.py:118
  138.8 1.5 %bitcast_convert_fusion = f32[1,32,1024]{2,1,0:T(8,128)} fusion(bf16[32,1024]{1,0:T(8,128)(2,1)} %reduce-scatter.2.cloned.1.call-done), kind=kLoop, calls=%fused_computation.40 | loop fusion | flops 32768 | bytes 196608 | tf_op jit(solution)/shard_map/broadcast_in_dim | solution.py:130
  (65 shorter events, 14.4 us)
Async XLA Ops:
  6.5 23.2 %copy-start = (bf16[1024,1024]{1,0:T(8,128)(2,1)S(1)}, bf16[1024,1024]{1,0:T(8,128)(2,1)}, u32[]{:S(2)}) copy-start(bf16[1024,1024]{1,0:T(8,128)(2,1)} %param.20) | copy-start | bytes 6291460
  27.0 0.8 copy-start.2
  29.2 2.4 %copy-start.1 = (f32[768,1024]{1,0:T(8,128)}, f32[768,1024]{1,0:T(8,128)S(1)}, u32[]{:S(2)}) copy-start(f32[768,1024]{1,0:T(8,128)S(1)} %get-tuple-element.55) | copy-start | bytes 9437188
  29.7 3.7 %copy-start.8 = (f32[1,112,768]{2,1,0:T(8,128)S(1)}, f32[1,112,768]{2,1,0:T(8,128)}, u32[]{:S(2)}) copy-start(f32[1,112,768]{2,1,0:T(8,128)} %param.16) | copy-start | bytes 1032196
  29.7 3.7 %copy-start.9 = (bf16[1024,112]{0,1:T(8,128)(2,1)S(1)}, bf16[1024,112]{0,1:T(8,128)(2,1)}, u32[]{:S(2)}) copy-start(bf16[1024,112]{0,1:T(8,128)(2,1)} %param.22) | copy-start | bytes 688132
  29.7 3.7 %copy-start.11 = (f32[1024]{0:T(1024)S(1)}, f32[1024]{0:T(1024)}, u32[]{:S(2)}) copy-start(f32[1024]{0:T(1024)} %param.21) | copy-start | bytes 12292
  29.8 3.6 %copy-start.13 = (f32[112]{0:T(128)S(1)}, f32[112]{0:T(128)}, u32[]{:S(2)}) copy-start(f32[112]{0:T(128)} %param.23) | copy-start | bytes 1348
  31.7 1.7 %copy-start.14 = (f32[768,1024]{1,0:T(8,128)}, f32[768,1024]{1,0:T(8,128)S(1)}, u32[]{:S(2)}) copy-start(f32[768,1024]{1,0:T(8,128)S(1)} %fusion.9) | copy-start | bytes 9437188
  33.4 10.7 %copy-start.5 = (f32[1,112,12]{1,0,2:T(1,128)S(1)}, f32[1,112,12]{1,0,2:T(1,128)}, u32[]{:S(2)}) copy-start(f32[1,112,12]{1,0,2:T(1,128)} %param.17) | copy-start | bytes 16132
  33.4 10.7 %copy-start.6 = (f32[112]{0:T(128)S(1)}, f32[112]{0:T(128)}, u32[]{:S(2)}) copy-start(f32[112]{0:T(128)} %param.19) | copy-start | bytes 1348
  33.4 10.7 %copy-start.7 = (f32[1,12]{1,0:T(1,128)S(1)}, f32[1,12]{1,0:T(1,128)}, u32[]{:S(2)}) copy-start(f32[1,12]{1,0:T(1,128)} %param.18) | copy-start | bytes 148
  35.5 18.0 %all-to-all-start = ((f32[1,112,768]{1,0,2:T(1,128)}), f32[1,112,768]{1,0,2:T(1,128)S(1)}, u32[]{:S(2)}, u32[]{:S(2)}) async-start(f32[1,112,768]{1,0,2:T(1,128)} %copy.34), calls=%async_computation | async-start | bytes 786432 | tf_op jit(solution)/shard_map/all_to_all | solution.py:80
  44.0 94.7 %reduce-scatter.2.cloned.1.call-start = ((), (), s32[]{:S(2)}) async-start(), calls=%async_computation.3 | async-start | bytes 327680 | tf_op jit(solution)/shard_map/reduce_scatter | solution.py:118
  82.7 6.7 %copy-start.4 = (f32[112,12]{0,1:T(8,128)S(1)}, f32[112,12]{0,1:T(8,128)}, u32[]{:S(2)}) copy-start(f32[112,12]{0,1:T(8,128)} %broadcast_multiply_fusion.1) | copy-start | bytes 16132
  86.7 16.8 %copy-start.10 = (bf16[1024,112]{0,1:T(8,128)(2,1)S(1)}, bf16[1024,112]{0,1:T(8,128)(2,1)}, u32[]{:S(2)}) copy-start(bf16[1024,112]{0,1:T(8,128)(2,1)} %param.22) | copy-start | bytes 688132
  86.7 16.8 %copy-start.12 = (f32[1024]{0:T(1024)S(1)}, f32[1024]{0:T(1024)}, u32[]{:S(2)}) copy-start(f32[1024]{0:T(1024)} %param.21) | copy-start | bytes 12292
  103.5 6.2 %copy-start.3 = (f32[768,128]{1,0:T(8,128)S(1)}, f32[768,128]{1,0:T(8,128)}, u32[]{:S(2)}) copy-start(f32[768,128]{1,0:T(8,128)} %copy-done.2) | copy-start | bytes 1179652
Sparse Core Ops, SparseCore 0:
  116.0 22.7 reduce-scatter.1
where the time goes:
time: 148 us; the launch traced here: 147 us
  local copies, waits for them, and re-layouts  34.9 us (24%)
  blocking collectives  31.8 us (21%)
  waiting for transfers between devices  31.7 us (21%)
  matrix products  16.8 us (11%)
  between operations  13.7 us (9%)
  other arithmetic  9.67 us (7%)
  starting transfers between devices  8.52 us (6%)
    reduce_scatter x1, waiting for transfers between devices, local(): lax.psum_scatter(lax.dot_general(matrix, grad_cell, (((0,), (0,)), ((), (...  22.9 us
    all_gather x1, blocking collectives, local(): shard_rows = lax.all_gather(mesh_local, 'shard', axis=0, tiled=True)  18.1 us
    all_to_all x1, blocking collectives, local(): lax.all_to_all(slopes, 'member', split_axis=0, concat_axis=2, tiled=True)[0]  13.7 us
    sub x17, local copies, waits for them, and re-layouts, group_pairs(): return jnp.sum(softened_slope(chosen[:, None] - flattened[None]), axis=1)  9.59 us
    all_to_all x1, waiting for transfers between devices, local(): lax.all_to_all(prediction_piece[None], 'member', split_axis=2, concat_axi...  8.79 us
    all_to_all x1, starting transfers between devices, local(): lax.all_to_all(prediction_piece[None], 'member', split_axis=2, concat_axi...  8.48 us
    mul x2, local copies, waits for them, and re-layouts, local(): (1.0 - fairness_factor) / (members - 1) * pairwise_sums  6.63 us
    dot_general x1, matrix products, local(): lax.dot_general(matrix, grad_cell, (((0,), (0,)), ((), ())), precision=la...  6.18 us
  transfers between devices with their start and end apart: 2, of which 2 were waited for; matrix products, arithmetic and copies ran while one was open for 0% of the time, Pallas kernels for 0%

commit v1 on v0

--- a/solution.py
+++ b/solution.py
@@ -56,7 +56,9 @@
     variables = previous.shape[0]
     members = lax.axis_size("member")
     block_cells = cell_count // members
-    shard_rows = lax.all_gather(mesh_local, "shard", axis=0, tiled=True)
+    shard_rows = jnp.concatenate(
+        lax.all_to_all(jnp.stack([mesh_local] * lax.axis_size("shard")), "shard", 0, 0), axis=0
+    )
     matrix = stencil_matrix(stencil, weights, shard_rows.shape[0])
     latent = jnp.dot(
         matrix,

time: 148 us -> 146 us (0.986)
  blocking collectives: 31.8 us -> 13.7 us
  starting transfers between devices: 8.52 us -> 16.7 us
  waiting for transfers between devices: 31.7 us -> 38.5 us
    all_gather x1 -> x0, blocking collectives: 18.1 us -> none  [local(): shard_rows = lax.all_gather(mesh_local, 'shard', axis=0, tiled=True)]
    all_to_all x0 -> x1, waiting for transfers between devices: none -> 8.53 us  [local(): lax.all_to_all(jnp.stack([mesh_local] * lax.axis_size('shard')), 'shard',...]
    all_to_all x0 -> x1, starting transfers between devices: none -> 8.46 us  [local(): lax.all_to_all(jnp.stack([mesh_local] * lax.axis_size('shard')), 'shard',...]
    another operation x0 -> x1, local copies, waits for them, and re-layouts: none -> 1.71 us  [local(): jnp.stack([mesh_local] * lax.axis_size('shard'))]
    reduce_scatter x1, waiting for transfers between devices: 22.9 us -> 21.2 us  [local(): lax.psum_scatter(lax.dot_general(matrix, grad_cell, (((0,), (0,)), ((), (...]
  transfers between devices with their start and end apart: 2 -> 3, of which waited for: 2 -> 3; matrix products, arithmetic and copies ran while one was open for 0% -> 2% of each run, Pallas kernels for 0% -> 0%
where the time goes in v1:
time: 146 us; the launch traced here: 145 us
  waiting for transfers between devices  38.5 us (26%)
  local copies, waits for them, and re-layouts  35.8 us (25%)
  starting transfers between devices  16.7 us (11%)
  matrix products  16.7 us (11%)
  blocking collectives  13.7 us (9%)
  between operations  13.7 us (9%)
  other arithmetic  9.67 us (7%)
    reduce_scatter x1, waiting for transfers between devices, local(): lax.psum_scatter(lax.dot_general(matrix, grad_cell, (((0,), (0,)), ((), (...  21.2 us
    all_to_all x1, blocking collectives, local(): lax.all_to_all(slopes, 'member', split_axis=0, concat_axis=2, tiled=True)[0]  13.7 us
    sub x17, local copies, waits for them, and re-layouts, group_pairs(): return jnp.sum(softened_slope(chosen[:, None] - flattened[None]), axis=1)  9.59 us
    all_to_all x1, waiting for transfers between devices, local(): lax.all_to_all(prediction_piece[None], 'member', split_axis=2, concat_axi...  8.79 us
    all_to_all x1, waiting for transfers between devices, local(): lax.all_to_all(jnp.stack([mesh_local] * lax.axis_size('shard')), 'shard',...  8.53 us
    all_to_all x1, starting transfers between devices, local(): lax.all_to_all(jnp.stack([mesh_local] * lax.axis_size('shard')), 'shard',...  8.46 us
    all_to_all x1, starting transfers between devices, local(): lax.all_to_all(prediction_piece[None], 'member', split_axis=2, concat_axi...  8.24 us
    mul x2, local copies, waits for them, and re-layouts, local(): (1.0 - fairness_factor) / (members - 1) * pairwise_sums  6.64 us
  transfers between devices with their start and end apart: 3, of which 3 were waited for; matrix products, arithmetic and copies ran while one was open for 2% of the time, Pallas kernels for 0%

profile of v1, /device:TPU:2, one launch (start us, length us, event | category | flops | bytes accessed | tf_op | source)
XLA Modules:
  0.0 144.9 jit_solution(5145250977044270354)
XLA Ops:
  6.5 1.7 %stack.3 = bf16[4,32,1024]{2,1,0:T(8,128)(2,1)} broadcast(bf16[32,1024]{1,0:T(8,128)(2,1)} %bitcast.69), dimensions={1,2} | broadcast | bytes 327680 | tf_op jit(solution)/shard_map/stack | solution.py:60
  8.2 8.5 %all-to-all-start = ((bf16[4,32,1024]{2,1,0:T(8,128)(2,1)}), bf16[4,32,1024]{2,1,0:T(8,128)(2,1)S(1)}, u32[]{:S(2)}, u32[]{:S(2)}) async-start(bf16[4,32,1024]{2,1,0:T(8,128)(2,1)} %stack.3), calls=%async_computation | async-start | bytes 524288 | tf_op jit(solution)/shard_map/all_to_all | solution.py:60
  18.1 0.8 select_reduce_fusion
  18.9 8.5 %all-to-all-done = bf16[4,32,1024]{2,1,0:T(8,128)(2,1)S(1)} async-done(((bf16[4,32,1024]{2,1,0:T(8,128)(2,1)}), bf16[4,32,1024]{2,1,0:T(8,128)(2,1)S(1)}, u32[]{:S(2)}, u32[]{:S(2)}) %all-to-all-start) | async-done | bytes 262176 | tf_op jit(solution)/shard_map/all_to_all | solution.py:60
  27.4 1.5 %fusion.29 = (f32[768]{0:T(1024)S(1)}, f32[768,1024]{1,0:T(8,128)S(1)}) fusion(f32[768,128]{1,0:T(8,128)S(1)} %select_reduce_fusion, bf16[128,1024]{1,0:T(8,128)(2,1)S(1)} %bitcast.67), kind=kOutput, calls=%fused_computation.50 | convolution fusion | flops 1208745216 | bytes 3804160 | tf_op jit(solution)/shard_map/dot_general | solution.py:63
  29.5 1.9 %fusion.9 = f32[768,1024]{1,0:T(8,128)S(1)} fusion(bf16[1024,1024]{1,0:T(8,128)(2,1)S(1)} %copy-done, f32[768,1024]{1,0:T(8,128)S(1)} %get-tuple-element.55, f32[768]{0:T(1024)S(1)} %add_rsqrt_fusion, f32[768]{0:T(1024)S(1)} %broadcast_multiply_fusion.4), kind=kOutput, calls=%fused_computation.19 | convolution fusion | flops 1612972032 | bytes 8394752 | tf_op jit(solution)/shard_map/dot_general | solution.py:29
  31.4 1.7 %copy-done.14 = f32[768,1024]{1,0:T(8,128)} copy-done((f32[768,1024]{1,0:T(8,128)}, f32[768,1024]{1,0:T(8,128)S(1)}, u32[]{:S(2)}) %copy-start.14) | copy-done | bytes 3145752
  33.1 1.1 fusion.25
  34.2 1.0 copy.34
  35.2 8.2 %all-to-all-start.1 = ((f32[1,112,768]{1,0,2:T(1,128)}), f32[1,112,768]{1,0,2:T(1,128)S(1)}, u32[]{:S(2)}, u32[]{:S(2)}) async-start(f32[1,112,768]{1,0,2:T(1,128)} %copy.34), calls=%async_computation.1 | async-start | bytes 786432 | tf_op jit(solution)/shard_map/all_to_all | solution.py:82
  44.2 8.8 %all-to-all-done.1 = f32[1,112,768]{1,0,2:T(1,128)S(1)} async-done(((f32[1,112,768]{1,0,2:T(1,128)}), f32[1,112,768]{1,0,2:T(1,128)S(1)}, u32[]{:S(2)}, u32[]{:S(2)}) %all-to-all-start.1) | async-done | bytes 344096 | tf_op jit(solution)/shard_map/all_to_all | solution.py:82
  53.0 3.3 %copy.36 = f32[64,1,112,12]{3,2,0,1:T(8,128)} copy(f32[64,1,112,12]{2,1,3,0:T(1,128)S(1)} %bitcast.62) | data formatting | bytes 688128 | tf_op jit(solution)/shard_map/all_to_all | solution.py:82
  56.3 1.3 copy.40
  57.6 3.8 %reshape_reshape.3 = f32[8,8,1344]{2,1,0:T(8,128)} reshape(f32[64,1,112,12]{3,2,0,1:T(8,128)} %copy.36) | data formatting | bytes 688128 | tf_op jit(solution)/shard_map/reshape;reshape | solution.py:88
  61.5 1.2 sub.126
  62.7 18.5 %while.11 = (s32[]{:T(128)}, f32[8,8,1344]{2,1,0:T(8,128)}, f32[8,8,1344]{2,1,0:T(8,128)}, f32[64,112,12]{0,2,1:T(8,128)}, f32[64,1344]{0,1:T(8,128)S(1)}, /*index=5*/s32[]{:T(128)}) while((s32[]{:T(128)}, f32[8,8,1344]{2,1,0:T(8,128)}, f32[8,8,1344]{2,1,0:T(8,128)}, f32[64,112,12]{0,2,1:T(8,128)}, f32[64,1344]{0,1:T(8,128)S(1)}, ...), condition=%wide.wide.region_5.6_spmd, body=%wide.wide.region_3.5_spmd.sunk | while | flops 3429890 | bytes 1292373 | solution.py:93
  63.0 0.8 dynamic-slice_bitcast_fusion.3
  65.3 0.8 dynamic-slice_bitcast_fusion.3
  67.6 0.8 dynamic-slice_bitcast_fusion.3
  69.9 0.8 dynamic-slice_bitcast_fusion.3
  72.2 0.8 dynamic-slice_bitcast_fusion.3
  74.5 0.8 dynamic-slice_bitcast_fusion.3
  76.8 0.8 dynamic-slice_bitcast_fusion.3
  79.1 0.8 dynamic-slice_bitcast_fusion.3
  81.2 1.0 broadcast_multiply_fusion
  82.2 3.9 %mul.93 = f32[64,112,12]{2,1,0:T(8,128)} reshape(f32[8,8,1344]{2,1,0:T(8,128)S(1)} %broadcast_multiply_fusion) | data formatting | bytes 688128 | tf_op jit(solution)/shard_map/mul | solution.py:99
  86.2 2.7 %copy.38 = f32[64,112,12]{1,0,2:T(8,128)S(1)} copy(f32[64,112,12]{2,1,0:T(8,128)} %mul.93) | data formatting | bytes 688128 | tf_op jit(solution)/shard_map/mul | solution.py:99
  89.2 13.7 %all_to_all.38 = bf16[64,112,12]{1,2,0:T(8,128)(2,1)S(1)} all-to-all(bf16[64,112,12]{1,2,0:T(8,128)(2,1)S(1)} %copy.39), channel_id=1, replica_groups=mesh['member'=64,'shard'=4] {'member'}, dimensions={0} | all-to-all | bytes 344064 | tf_op jit(solution)/shard_map/all_to_all | solution.py:102
  103.0 6.1 %fusion.28 = (f32[768]{0:T(1024)S(1)}, f32[768]{0:T(1024)S(1)}, f32[768,1024]{1,0:T(8,128)}) fusion(f32[768]{0:T(1024)S(1)} %add_rsqrt_fusion, f32[768,1024]{1,0:T(8,128)} %copy-done.1, f32[768]{0:T(1024)S(1)} %broadcast_multiply_fusion.4, bf16[1024,1024]{1,0:T(8,128)(2,1)S(1)} %copy-done, f32[768,1024]{1,0:T(8,128)} %copy-done.14, ...), kind=kOutput, calls=%fused_computation.49 | convolution fusion | flops 1798568448 | bytes 11952128 | tf_op jit(solution)/shard_map/dot_general | solution.py:111
  109.1 6.2 %fusion.19 = bf16[128,1024]{1,0:T(8,128)(2,1)} fusion(f32[768,128]{1,0:T(8,128)S(1)} %copy-done.3, f32[768,1024]{1,0:T(8,128)} %get-tuple-element.56, f32[768,1024]{1,0:T(8,128)} %copy-done.1, f32[768]{0:T(1024)S(1)} %get-tuple-element.57, f32[768]{0:T(1024)S(1)} %get-tuple-element.58, f32[768]{0:T(1024)S(1)} %add_rsqrt_fusion, ...), kind=kOutput, calls=%fused_computation.28 | convolution fusion | flops 1212809216 | bytes 6959104 | tf_op jit(solution)/shard_map/dot_general | solution.py:121
  115.4 21.2 %reduce-scatter.2.cloned.1.call-done = bf16[32,1024]{1,0:T(8,128)(2,1)} async-done(((bf16[128,1024]{1,0:T(8,128)(2,1)}), bf16[32,1024]{1,0:T(8,128)(2,1)}) %reduce-scatter.2.cloned.1.call-update) | async-done | bytes 65552 | tf_op jit(solution)/shard_map/reduce_scatter | solution.py:120
  136.6 1.5 %bitcast_convert_fusion = f32[1,32,1024]{2,1,0:T(8,128)} fusion(bf16[32,1024]{1,0:T(8,128)(2,1)} %reduce-scatter.2.cloned.1.call-done), kind=kLoop, calls=%fused_computation.38 | loop fusion | flops 32768 | bytes 196608 | tf_op jit(solution)/shard_map/broadcast_in_dim | solution.py:132
  (67 shorter events, 15.1 us)
Async XLA Ops:
  6.5 22.9 %copy-start = (bf16[1024,1024]{1,0:T(8,128)(2,1)S(1)}, bf16[1024,1024]{1,0:T(8,128)(2,1)}, u32[]{:S(2)}) copy-start(bf16[1024,1024]{1,0:T(8,128)(2,1)} %param.20) | copy-start | bytes 6291460
  8.2 19.2 %all-to-all-start = ((bf16[4,32,1024]{2,1,0:T(8,128)(2,1)}), bf16[4,32,1024]{2,1,0:T(8,128)(2,1)S(1)}, u32[]{:S(2)}, u32[]{:S(2)}) async-start(bf16[4,32,1024]{2,1,0:T(8,128)(2,1)} %stack.3), calls=%async_computation | async-start | bytes 524288 | tf_op jit(solution)/shard_map/all_to_all | solution.py:60
  18.9 10.5 %copy-start.2 = (f32[768,128]{1,0:T(8,128)}, f32[768,128]{1,0:T(8,128)S(1)}, u32[]{:S(2)}) copy-start(f32[768,128]{1,0:T(8,128)S(1)} %select_reduce_fusion) | copy-start | bytes 1179652
  28.9 2.4 %copy-start.1 = (f32[768,1024]{1,0:T(8,128)}, f32[768,1024]{1,0:T(8,128)S(1)}, u32[]{:S(2)}) copy-start(f32[768,1024]{1,0:T(8,128)S(1)} %get-tuple-element.55) | copy-start | bytes 9437188
  29.4 3.7 %copy-start.8 = (f32[1,112,768]{2,1,0:T(8,128)S(1)}, f32[1,112,768]{2,1,0:T(8,128)}, u32[]{:S(2)}) copy-start(f32[1,112,768]{2,1,0:T(8,128)} %param.16) | copy-start | bytes 1032196
  29.4 3.7 %copy-start.9 = (bf16[1024,112]{0,1:T(8,128)(2,1)S(1)}, bf16[1024,112]{0,1:T(8,128)(2,1)}, u32[]{:S(2)}) copy-start(bf16[1024,112]{0,1:T(8,128)(2,1)} %param.22) | copy-start | bytes 688132
  29.4 3.6 %copy-start.11 = (f32[1024]{0:T(1024)S(1)}, f32[1024]{0:T(1024)}, u32[]{:S(2)}) copy-start(f32[1024]{0:T(1024)} %param.21) | copy-start | bytes 12292
  29.5 3.6 %copy-start.13 = (f32[112]{0:T(128)S(1)}, f32[112]{0:T(128)}, u32[]{:S(2)}) copy-start(f32[112]{0:T(128)} %param.23) | copy-start | bytes 1348
  31.4 1.7 %copy-start.14 = (f32[768,1024]{1,0:T(8,128)}, f32[768,1024]{1,0:T(8,128)S(1)}, u32[]{:S(2)}) copy-start(f32[768,1024]{1,0:T(8,128)S(1)} %fusion.9) | copy-start | bytes 9437188
  33.1 10.4 %copy-start.5 = (f32[1,112,12]{1,0,2:T(1,128)S(1)}, f32[1,112,12]{1,0,2:T(1,128)}, u32[]{:S(2)}) copy-start(f32[1,112,12]{1,0,2:T(1,128)} %param.17) | copy-start | bytes 16132
  33.1 10.4 %copy-start.6 = (f32[112]{0:T(128)S(1)}, f32[112]{0:T(128)}, u32[]{:S(2)}) copy-start(f32[112]{0:T(128)} %param.19) | copy-start | bytes 1348
  33.1 10.4 %copy-start.7 = (f32[1,12]{1,0:T(1,128)S(1)}, f32[1,12]{1,0:T(1,128)}, u32[]{:S(2)}) copy-start(f32[1,12]{1,0:T(1,128)} %param.18) | copy-start | bytes 148
  35.2 17.8 %all-to-all-start.1 = ((f32[1,112,768]{1,0,2:T(1,128)}), f32[1,112,768]{1,0,2:T(1,128)S(1)}, u32[]{:S(2)}, u32[]{:S(2)}) async-start(f32[1,112,768]{1,0,2:T(1,128)} %copy.34), calls=%async_computation.1 | async-start | bytes 786432 | tf_op jit(solution)/shard_map/all_to_all | solution.py:82
  43.5 93.1 %reduce-scatter.2.cloned.1.call-start = ((), (), s32[]{:S(2)}) async-start(), calls=%async_computation.4 | async-start | bytes 327680 | tf_op jit(solution)/shard_map/reduce_scatter | solution.py:120
  82.2 6.7 %copy-start.4 = (f32[112,12]{0,1:T(8,128)S(1)}, f32[112,12]{0,1:T(8,128)}, u32[]{:S(2)}) copy-start(f32[112,12]{0,1:T(8,128)} %broadcast_multiply_fusion.1) | copy-start | bytes 16132
  86.2 16.8 %copy-start.10 = (bf16[1024,112]{0,1:T(8,128)(2,1)S(1)}, bf16[1024,112]{0,1:T(8,128)(2,1)}, u32[]{:S(2)}) copy-start(bf16[1024,112]{0,1:T(8,128)(2,1)} %param.22) | copy-start | bytes 688132
  86.2 16.8 %copy-start.12 = (f32[1024]{0:T(1024)S(1)}, f32[1024]{0:T(1024)}, u32[]{:S(2)}) copy-start(f32[1024]{0:T(1024)} %param.21) | copy-start | bytes 12292
  103.0 6.1 %copy-start.3 = (f32[768,128]{1,0:T(8,128)S(1)}, f32[768,128]{1,0:T(8,128)}, u32[]{:S(2)}) copy-start(f32[768,128]{1,0:T(8,128)} %copy-done.2) | copy-start | bytes 1179652
Sparse Core Ops, SparseCore 0:
  115.5 21.0 reduce-scatter.1
